TPU v7x, 256 devices: a whole 4x4x8 slice. The times are simulated.
256 devices in a mesh: item: 32 (over x, z), day: 8 (over y, core).
Axes of the slice: x: 4, y: 4, z: 8, core: 2. Of those that a mesh axis runs over, the one named last changes fastest.
Arguments:
- user_factors: float32 [2048, 512], P(('item', 'day')), may hold values from 0.005 to 0.012
- item_factors: bfloat16 [16384, 512], P('item'), may hold values from 0 to 1
- day_factors: bfloat16 [368, 512], P('day'), may hold values from 0.099609375 to 1
- tile_counts: bfloat16 [32768, 128, 128], P(('item', 'day')), may hold values from 0 to 23
- tile_index: int32 [3, 32768], P(None, ('item', 'day')), may hold values from 0 to 45, as said below
- tile_live: int32 [256], P(('item', 'day')), may hold values from 32 to 128, as said below
Outputs:
- updated_users: float32 [2048, 512], P(('item', 'day'))
Inputs may be any that keep to these rules, and one draw needn't show every extreme that they name: `tile_index`: row 0 names a user block below 16, row 1 an item block below 4 and row 2 a day below 46, local to the device that holds the slot. Only the first tile_live[d] slots of list d are live; some list has all 128 live.
All inputs are finite; a program needn't handle non-finite values.
Results may differ from a plain program's by a relative error of at most 0.003.
Values may be sent and summed in bfloat16 or wider, within the bound.
A program may use at most 64 MiB of HBM per device.

v0:
```python
import jax
import jax.numpy as jnp
from jax import lax
from jax.sharding import PartitionSpec as P

TILE = 128
GROUP = 8


def group_turns(phi, user_blocks, item_blocks, day_rows, counts, index, low, high):

    def turn(step, phi):
        start = step * GROUP
        tile_vals = lax.dynamic_slice_in_dim(counts, start, GROUP, 0)
        picks = lax.dynamic_slice_in_dim(index, start, GROUP, 1)
        places = start + jnp.arange(GROUP, dtype=jnp.int32)
        active = (places >= low) & (places < high)
        users = user_blocks[picks[0]]
        items = item_blocks[picks[1]]
        scales = day_rows[picks[2]].astype(jnp.float32)[:, None, :]
        scaled = (users.astype(jnp.float32) * scales).astype(jnp.bfloat16)
        model = jnp.einsum("gur,gir->gui", scaled, items, preferred_element_type=jnp.float32)
        ratio = jnp.where(active[:, None, None], tile_vals.astype(jnp.float32) / model, 0.0).astype(
            jnp.bfloat16
        )
        weighted = (items.astype(jnp.float32) * scales).astype(jnp.bfloat16)
        terms = jnp.einsum("gui,gir->gur", ratio, weighted, preferred_element_type=jnp.float32)
        return phi.at[picks[0]].add(terms)

    first = jnp.maximum(low, 0) // GROUP
    last = jnp.maximum((high + GROUP - 1) // GROUP, first)
    return lax.fori_loop(first, last, turn, phi)


def per_device(user_factors, item_factors, day_factors, tile_counts, tile_index, tile_live):
    rank = user_factors.shape[1]
    gathered = lax.all_gather(
        user_factors.astype(jnp.bfloat16), ("item", "day"), axis=0, tiled=True
    )
    user_blocks = gathered.reshape(-1, TILE, rank)
    item_blocks = item_factors.reshape(-1, TILE, rank)
    phi = jnp.zeros(user_blocks.shape, jnp.float32)
    own_count = tile_live[0]
    phi = group_turns(
        phi, user_blocks, item_blocks, day_factors, tile_counts, tile_index, 0, own_count
    )
    owned = lax.psum_scatter(
        phi.reshape(-1, rank), ("item", "day"), scatter_dimension=0, tiled=True
    )
    item_total = lax.psum(jnp.sum(item_factors.astype(jnp.float32), axis=0), "item")
    day_total = lax.psum(jnp.sum(day_factors.astype(jnp.float32), axis=0), "day")
    return user_factors * owned / (item_total * day_total)


def solution(mesh):
    in_specs = (
        P(("item", "day"), None),
        P("item", None),
        P("day", None),
        P(("item", "day"), None, None),
        P(None, ("item", "day")),
        P(("item", "day")),
    )
    out_specs = P(("item", "day"), None)
    return jax.shard_map(
        per_device, mesh=mesh, in_specs=in_specs, out_specs=out_specs, check_vma=False
    )
```

profile of v0, /device:TPU:0, one launch (start us, length us, event | category | flops | bytes accessed | tf_op | source)
XLA Modules:
  0.0 1606.9 jit_solution(8117053464810953249)
XLA Ops:
  6.5 1.3 convert_element_type.34
  8.6 107.7 %all-gather.2.cloned.1.call-done = bf16[2048,512]{1,0:T(8,128)(2,1)} async-done(((bf16[8,512]{1,0:T(8,128)(2,1)}), bf16[2048,512]{1,0:T(8,128)(2,1)}) %all-gather.2.cloned.1.call-update) | async-done | bytes 2097168 | tf_op jit(solution)/shard_map/all_gather | solution.py:37
  116.3 2.5 broadcast_in_dim.14
  118.7 78.3 %while.10 = (s32[]{:T(128)}, f32[16,128,512]{2,1,0:T(8,128)}, s32[]{:T(128)}, s32[3,128]{1,0:T(4,128)S(1)}, s32[]{:T(128)}, /*index=5*/bf16[128,128,128]{2,1,0:T...) while((s32[]{:T(128)}, f32[16,128,512]{2,1,0:T(8,128)}, ...), condition=%wide.region_2.3_spmd, body=%wide.region_0.2_spmd.sunk | while | flops 272637024 | bytes 16078115 | solution.py:32
  118.9 1.6 gather_fusion
  121.1 3.2 gather_fusion.1
  124.9 2.7 fusion.20
  127.6 4.2 scatter_fusion
  131.9 1.6 gather_fusion
  134.1 3.2 gather_fusion.1
  137.9 2.7 fusion.20
  140.6 4.2 scatter_fusion
  144.9 1.6 gather_fusion
  147.1 3.2 gather_fusion.1
  151.0 2.7 fusion.20
  153.7 4.3 scatter_fusion
  158.1 1.6 gather_fusion
  160.3 3.2 gather_fusion.1
  164.1 2.7 fusion.20
  166.8 4.2 scatter_fusion
  171.1 1.6 gather_fusion
  173.3 3.2 gather_fusion.1
  177.2 2.7 fusion.20
  179.9 4.1 scatter_fusion
  184.1 1.6 gather_fusion
  186.3 3.2 gather_fusion.1
  190.1 2.7 fusion.20
  192.8 4.2 scatter_fusion
  197.1 183.4 %psum.14 = f32[512]{0:T(512)S(1)} all-reduce(f32[512]{0:T(512)S(1)} %convert_reduce_fusion), channel_id=1, replica_groups=mesh['item'=32,'day'=8] {'item'}, use_global_device_ids=true, to_apply=%region_5.6 | all-reduce | flops 512 | bytes 4096 | tf_op jit(solution)/shard_map/psum | solution.py:50
  380.5 12.4 psum.15
  393.0 1205.8 %reduce-scatter.2.cloned.1.call-done = f32[8,512]{1,0:T(8,128)} async-done(((f32[2048,512]{1,0:T(8,128)}), f32[8,512]{1,0:T(8,128)}) %reduce-scatter.2.cloned.1.call-update) | async-done | bytes 16400 | tf_op jit(solution)/shard_map/reduce_scatter | solution.py:47
  1598.7 1.3 multiply_divide_fusion
  (57 shorter events, 8.1 us)
Async XLA Ops:
  6.5 109.7 %all-gather.2.cloned.1.call-start = ((), (), s32[]{:S(2)}) async-start(), calls=%async_computation.1 | async-start | bytes 2105344 | tf_op jit(solution)/shard_map/all_gather | solution.py:37
  7.9 1590.9 %reduce-scatter.2.cloned.1.call-start = ((), (), s32[]{:S(2)}) async-start(), calls=%async_computation.2 | async-start | bytes 4210688 | tf_op jit(solution)/shard_map/reduce_scatter | solution.py:47
  116.3 2.5 copy-start
  116.3 2.5 copy-start.1
  116.3 2.5 copy-start.3
  197.0 1401.7 %copy-start.2 = (f32[8,512]{1,0:T(8,128)S(1)}, f32[8,512]{1,0:T(8,128)}, u32[]{:S(2)}) copy-start(f32[8,512]{1,0:T(8,128)} %param.8) | copy-start | bytes 49156
Sparse Core Ops, SparseCore 0:
  11.1 105.1 all-gather.1
  197.1 1401.5 reduce-scatter.1
where the time goes:
time: 1610 us
  waiting for transfers between devices  1310 us (81%)
  blocking collectives  196 us (12%)
  local copies, waits for them, and re-layouts  35.1 us (2%)
  other arithmetic  32.1 us (2%)
  matrix products  16.1 us (1%)
    reduce_scatter x1, waiting for transfers between devices, per_device(): lax.psum_scatter(phi.reshape(-1, rank), ('item', 'day'), scatter_dimensio...  1210 us
    psum x1, blocking collectives, per_device(): lax.psum(jnp.sum(item_factors.astype(jnp.float32), axis=0), 'item')  183 us
    all_gather x1, waiting for transfers between devices, per_device(): lax.all_gather(user_factors.astype(jnp.bfloat16), ('item', 'day'), axis=0...  108 us
  transfers between devices with their start and end apart: 2, of which 2 were waited for; matrix products, arithmetic and copies ran while one was open for 0% of the time, Pallas kernels for 0%

commit v1 on v0

v1 whole, which is shorter than its diff:
```python
import functools

import jax
import jax.numpy as jnp
from jax import lax
from jax.experimental import pallas as pl
from jax.experimental.pallas import tpu as pltpu
from jax.sharding import PartitionSpec as P

MESH = pl.DeviceIdType.MESH
R = 512
TILE = 128
CAP = 128
USER_BLOCKS = 16
DAY_DEV = 46
ITEMBLK_DEV = 4
NX, NY, NZ, NC = 4, 4, 8, 2
ROWS = 8
FOUR = 4
ORDER = CAP + USER_BLOCKS * (FOUR - 1)


def place():
    item, day = lax.axis_index("item"), lax.axis_index("day")
    x, z = lax.div(item, NZ), lax.rem(item, NZ)
    y, c = lax.div(day, NC), lax.rem(day, NC)
    return x, y, z, c


def device(x, y, z, c):
    return (x * NZ + z, y * NC + c)


def pick(c, zero, one):
    return zero + c * (one - zero)


def along(first, me, step):
    x, y, z, c = me
    return device(
        pick(first, lax.rem(x + step, NX), x), pick(first, y, lax.rem(y + step, NY)), z, c
    )


def greet(me, c):
    x, y, z, _ = me
    barrier = pltpu.get_barrier_semaphore()
    for step in range(1, NZ):
        pl.semaphore_signal(
            barrier, inc=1, device_id=device(x, y, lax.rem(z + step, NZ), c), device_id_type=MESH
        )
    for step in range(1, NX):
        for first in (0, 1):
            pl.semaphore_signal(
                barrier, inc=1, device_id=along(first, me, step), device_id_type=MESH
            )
    pl.semaphore_signal(barrier, inc=1, device_id=device(x, y, z, 1 - c), device_id_type=MESH)
    pl.semaphore_wait(barrier, NZ - 1 + 2 * (NX - 1) + 1)


def send(src, dst, sems, spot, target):
    copy = pltpu.make_async_remote_copy(
        src_ref=src,
        dst_ref=dst,
        send_sem=sems[0].at[spot],
        recv_sem=sems[1].at[spot],
        device_id=target,
        device_id_type=MESH,
    )
    copy.start()
    return copy


def gather_kernel(
    user_ref, item_ref, day_ref, all_ref, total_ref,
    sums, sums_z, sums_a, sums_b, sums_c,
    z_s, z_r, a_s, a_r, b_s, b_r, c_s, c_r, tz_s, tz_r, ta_s, ta_r, tb_s, tb_r, tc_s, tc_r,
):
    me = place()
    x, y, z, c = me
    a, b = pick(c, x, y), pick(c, y, x)
    all_ref[c, a, b, z] = user_ref[...].astype(jnp.bfloat16)
    item_sum = jnp.sum(item_ref[...].astype(jnp.float32), axis=0, keepdims=True)
    day_sum = jnp.sum(day_ref[...].astype(jnp.float32), axis=0, keepdims=True)
    for part in range(R // 128):
        lanes = slice(part * 128, (part + 1) * 128)
        sums[part : part + 1, :] = item_sum[:, lanes]
        sums[part + 4 : part + 5, :] = day_sum[:, lanes]
    greet(me, c)

    copies = []
    spot = all_ref.at[c, a, b, z]
    for step in range(1, NZ):
        target = device(x, y, lax.rem(z + step, NZ), c)
        copies.append(send(spot, spot, (z_s, z_r), step - 1, target))
        copies.append(send(sums, sums_z.at[step - 1], (tz_s, tz_r), step - 1, target))
    for copy in copies:
        copy.wait()
    sums[...] += jnp.sum(sums_z[...], axis=0)

    copies = []
    spot = all_ref.at[c, a, b]
    for step in range(1, NX):
        target = along(c, me, step)
        copies.append(send(spot, spot, (a_s, a_r), step - 1, target))
        copies.append(send(sums, sums_a.at[step - 1], (ta_s, ta_r), step - 1, target))
    for copy in copies:
        copy.wait()
    sums[...] += jnp.sum(sums_a[...], axis=0)

    copies = []
    spot = all_ref.at[c, :, b]
    for step in range(1, NX):
        target = along(1 - c, me, step)
        copies.append(send(spot, spot, (b_s, b_r), step - 1, target))
        copies.append(send(sums, sums_b.at[step - 1], (tb_s, tb_r), step - 1, target))
    other = device(x, y, z, 1 - c)
    passed = [send(spot, spot, (c_s, c_r), 0, other)]
    for step in range(1, NX):
        arrived = all_ref.at[c, :, lax.rem(b - step + NX, NX)]
        copies[2 * step - 2].wait()
        passed.append(send(arrived, arrived, (c_s, c_r), step, other))
    for step in range(1, NX):
        copies[2 * step - 1].wait()
    sums[...] += jnp.sum(sums_b[...], axis=0)
    passed.append(send(sums, sums_c, (tc_s, tc_r), 0, other))
    for copy in passed:
        copy.wait()
    total_ref[...] = sums[...] + sums_c[...]


def gather_call(user_factors, item_factors, day_factors):
    dma = pltpu.SemaphoreType.DMA
    vmem = pl.BlockSpec(memory_space=pltpu.VMEM)
    tile = (8, 128)
    return pl.pallas_call(
        gather_kernel,
        out_shape=(
            jax.ShapeDtypeStruct((NC, NX, NY, NZ, ROWS, R), jnp.bfloat16),
            jax.ShapeDtypeStruct(tile, jnp.float32),
        ),
        in_specs=[vmem] * 3,
        out_specs=(vmem, vmem),
        scratch_shapes=[
            pltpu.VMEM(tile, jnp.float32),
            pltpu.VMEM((NZ - 1,) + tile, jnp.float32),
            pltpu.VMEM((NX - 1,) + tile, jnp.float32),
            pltpu.VMEM((NX - 1,) + tile, jnp.float32),
            pltpu.VMEM(tile, jnp.float32),
        ]
        + [dma((NZ - 1,))] * 2 + [dma((NX - 1,))] * 4 + [dma((NX,))] * 2
        + [dma((NZ - 1,))] * 2 + [dma((NX - 1,))] * 4 + [dma((1,))] * 2,
        compiler_params=pltpu.CompilerParams(collective_id=0, has_side_effects=True),
        name="gather_users",
    )(user_factors, item_factors, day_factors)


def phi_kernel(
    index_ref, live_ref, all_ref, item_ref, day_ref, counts_ref, phi_ref,
    users, scales, w_even, w_odd, m_even, m_odd, order, cursor, sem,
):
    copies = []
    for a in range(NX):
        for b in range(NX):
            for c in range(NC):
                x, y = (a, b) if c == 0 else (b, a)
                copies.append(
                    pltpu.make_async_copy(
                        all_ref.at[c, a, b],
                        users.at[pl.ds(x * NZ, NZ), pl.ds(y * NC * ROWS + c * ROWS, ROWS)],
                        sem.at[c, a, b],
                    )
                )
    for copy in copies:
        copy.start()
    live = live_ref[0]

    for block in range(USER_BLOCKS):
        cursor[block] = 0

    def count(slot, carry):
        block = index_ref[0, slot]
        cursor[block] = cursor[block] + 1
        return carry

    lax.fori_loop(0, live, count, 0)
    start = jnp.int32(0)
    for block in range(USER_BLOCKS):
        turns = lax.div(cursor[block] + (FOUR - 1), FOUR)
        cursor[block] = start
        start = start + turns * FOUR
    groups = lax.div(start, FOUR)

    def clear(spot, carry):
        order[spot] = -1
        return carry

    lax.fori_loop(0, start + 2 * FOUR, clear, 0)

    def put(slot, carry):
        block = index_ref[0, slot]
        spot = cursor[block]
        order[spot] = slot
        cursor[block] = spot + 1
        return carry

    lax.fori_loop(0, live, put, 0)

    day_rows = day_ref[...].astype(jnp.float32)
    for day in range(DAY_DEV):
        scales[day] = jnp.broadcast_to(day_rows[day : day + 1], (16, R)).astype(jnp.bfloat16)
    phi_ref[...] = jnp.zeros_like(phi_ref)
    for copy in copies:
        copy.wait()

    def slots(group):
        return [order[group * FOUR + part] for part in range(FOUR)]

    def forward(group, w, m):
        for part, slot in enumerate(slots(group)):
            slot = jnp.maximum(slot, 0)
            items = item_ref[index_ref[1, slot]].reshape(TILE // 16, 16, R)
            scaled = items * scales[index_ref[2, slot]][None]
            w[part * TILE : (part + 1) * TILE, :] = scaled.reshape(TILE, R)
        block = index_ref[0, jnp.maximum(order[group * FOUR], 0)]
        rows = users[pl.ds(2 * block, 2)].reshape(TILE, R)
        m[...] = lax.dot_general(
            rows, w[...], (((1,), (1,)), ((), ())), preferred_element_type=jnp.float32
        )

    def backward(group, w, m):
        ratios = []
        for part, slot in enumerate(slots(group)):
            tile = counts_ref[jnp.maximum(slot, 0)].astype(jnp.float32)
            ratio = tile / m[:, part * TILE : (part + 1) * TILE]
            ratios.append(jnp.where(slot >= 0, ratio, 0.0).astype(jnp.bfloat16))
        block = index_ref[0, jnp.maximum(order[group * FOUR], 0)]
        phi_ref[block] += jnp.dot(
            jnp.concatenate(ratios, axis=1), w[...], preferred_element_type=jnp.float32
        )

    forward(0, w_even, m_even)

    def turn(pair, carry):
        group = 2 * pair
        forward(group + 1, w_odd, m_odd)
        backward(group, w_even, m_even)
        forward(group + 2, w_even, m_even)
        backward(group + 1, w_odd, m_odd)
        return carry

    lax.fori_loop(0, lax.div(groups + 1, 2), turn, 0)


def phi_call(tile_index, tile_live, everyone, item_factors, day_factors, tile_counts):
    smem = pl.BlockSpec(memory_space=pltpu.SMEM)
    vmem = pl.BlockSpec(memory_space=pltpu.VMEM)
    w = pltpu.VMEM((FOUR * TILE, R), jnp.bfloat16)
    m = pltpu.VMEM((TILE, FOUR * TILE), jnp.float32)
    return pl.pallas_call(
        phi_kernel,
        out_shape=jax.ShapeDtypeStruct((USER_BLOCKS, TILE, R), jnp.float32),
        in_specs=[smem, smem, pl.BlockSpec(memory_space=pl.ANY), vmem, vmem, vmem],
        out_specs=vmem,
        scratch_shapes=[
            pltpu.VMEM((NX * NZ, NY * NC * ROWS, R), jnp.bfloat16),
            pltpu.VMEM((DAY_DEV, 16, R), jnp.bfloat16),
            w, w, m, m,
            pltpu.SMEM((ORDER + 4 * FOUR,), jnp.int32),
            pltpu.SMEM((USER_BLOCKS,), jnp.int32),
            pltpu.SemaphoreType.DMA((NC, NX, NX)),
        ],
        compiler_params=pltpu.CompilerParams(vmem_limit_bytes=40 << 20),
        name="tile_turns",
    )(tile_index, tile_live, everyone, item_factors, day_factors, tile_counts)


def scatter_kernel(
    phi_ref, user_ref, total_ref, out_ref,
    own, other, near, far, deep,
    own_sem, o_s, o_r, n_s, n_r, f_s, f_r, d_s, d_r,
):
    me = place()
    x, y, z, c = me
    p, q = pick(c, y, x), pick(c, x, y)
    pairs = [(kp, kq) for kq in (1, 2, 3, 0) for kp in (1, 2, 3, 0)]

    def mine(kp, kq):
        return lax.rem(p + kp, NX), lax.rem(q + kq, NX)

    locals_ = {}
    for kp, kq in pairs:
        pp, qq = mine(kp, kq)
        locals_[kp, kq] = pltpu.make_async_copy(
            phi_ref.at[pick(c, qq, pp), :, pick(c, pp, qq), c], own.at[kp, kq], own_sem.at[kp, kq]
        )
        locals_[kp, kq].start()
    greet(me, c)
    sibling = device(x, y, z, 1 - c)
    crossed = {}
    for kp, kq in pairs:
        pp, qq = lax.rem(q + kp, NX), lax.rem(p + kq, NX)
        src = phi_ref.at[pick(c, pp, qq), :, pick(c, qq, pp), 1 - c]
        crossed[kp, kq] = send(src, other.at[kp, kq], (o_s, o_r), (kp, kq), sibling)

    nears = {}
    fars = {}
    for kq in (1, 2, 3, 0):
        for kp in (1, 2, 3, 0):
            locals_[kp, kq].wait()
            crossed[kp, kq].wait()
            own[kp, kq] += other[kp, kq]
            if kp:
                nears[kp, kq] = send(
                    own.at[kp, kq], near.at[kp - 1, kq], (n_s, n_r), (kp - 1, kq),
                    along(1 - c, me, kp),
                )
    for kq in (1, 2, 3, 0):
        for kp in (1, 2, 3):
            nears[kp, kq].wait()
        own[0, kq] += near[0, kq] + near[1, kq] + near[2, kq]
        if kq:
            fars[kq] = send(
                own.at[0, kq], far.at[kq - 1], (f_s, f_r), kq - 1, along(c, me, kq)
            )
    for kq in (1, 2, 3):
        fars[kq].wait()
    own[0, 0] += far[0] + far[1] + far[2]
    deeps = []
    for step in range(1, NZ):
        there = lax.rem(z + step, NZ)
        deeps.append(
            send(own.at[0, 0, there], deep.at[step - 1], (d_s, d_r), step - 1,
                 device(x, y, there, c))
        )
    totals = total_ref[0:4, :] * total_ref[4:8, :] * (1.0 / (NX * NZ * NY * NC))
    for copy in deeps:
        copy.wait()
    summed = own[0, 0, z] + jnp.sum(deep[...], axis=0)
    for part in range(R // 128):
        lanes = slice(part * 128, (part + 1) * 128)
        out_ref[:, lanes] = user_ref[:, lanes] * summed[:, lanes] / totals[part : part + 1, :]


def scatter_call(phi, user_factors, totals):
    dma = pltpu.SemaphoreType.DMA
    vmem = pl.BlockSpec(memory_space=pltpu.VMEM)
    piece = (NZ, ROWS, R)
    return pl.pallas_call(
        scatter_kernel,
        out_shape=jax.ShapeDtypeStruct((ROWS, R), jnp.float32),
        in_specs=[pl.BlockSpec(memory_space=pl.ANY), vmem, vmem],
        out_specs=vmem,
        scratch_shapes=[
            pltpu.VMEM((NX, NX) + piece, jnp.float32),
            pltpu.VMEM((NX, NX) + piece, jnp.float32),
            pltpu.VMEM((NX - 1, NX) + piece, jnp.float32),
            pltpu.VMEM((NX - 1,) + piece, jnp.float32),
            pltpu.VMEM((NZ - 1, ROWS, R), jnp.float32),
            dma((NX, NX)), dma((NX, NX)), dma((NX, NX)),
            dma((NX - 1, NX)), dma((NX - 1, NX)),
            dma((NX - 1,)), dma((NX - 1,)),
            dma((NZ - 1,)), dma((NZ - 1,)),
        ],
        compiler_params=pltpu.CompilerParams(
            collective_id=1, has_side_effects=True, vmem_limit_bytes=24 << 20
        ),
        name="sum_phi",
    )(phi, user_factors, totals)


def per_device(user_factors, item_factors, day_factors, tile_counts, tile_index, tile_live):
    everyone, totals = gather_call(user_factors, item_factors, day_factors)
    phi = phi_call(
        tile_index, tile_live, everyone,
        item_factors.reshape(ITEMBLK_DEV, TILE, R), day_factors, tile_counts,
    )
    return scatter_call(phi.reshape(NX, NZ, NY, NC, ROWS, R), user_factors, totals)


def solution(mesh):
    in_specs = (
        P(("item", "day"), None),
        P("item", None),
        P("day", None),
        P(("item", "day"), None, None),
        P(None, ("item", "day")),
        P(("item", "day")),
    )
    out_specs = P(("item", "day"), None)
    return jax.shard_map(
        per_device, mesh=mesh, in_specs=in_specs, out_specs=out_specs, check_vma=False
    )
```

time: 1610 us -> 84.9 us (0.05)
  the two profiles are of different devices: /device:TPU:0 before, /device:TPU:6 now
where the time goes in v1:
time: 84.9 us; the launch traced here: 83.3 us
  Pallas kernels  75.7 us (89%)
  local copies, waits for them, and re-layouts  6.91 us (8%)
    pallas_call x1, Pallas kernels, gather_call(): pl.pallas_call(gather_kernel, out_shape=(jax.ShapeDtypeStruct((NC, NX, NY...  34.3 us
    pallas_call x1, Pallas kernels, scatter_call(): pl.pallas_call(scatter_kernel, out_shape=jax.ShapeDtypeStruct((ROWS, R),...  32 us
    pallas_call x1, Pallas kernels, phi_call(): pl.pallas_call(phi_kernel, out_shape=jax.ShapeDtypeStruct((USER_BLOCKS, T...  9.39 us
    unnamed x15, local copies, waits for them, and re-layouts  6.91 us

profile of v1, /device:TPU:6, one launch (start us, length us, event | category | flops | bytes accessed | tf_op | source)
XLA Modules:
  0.0 83.3 jit_solution(2735949402940224127)
XLA Ops:
  0.7 34.3 %gather_users.1 = (bf16[2,4,4,8,8,512]{5,4,3,2,1,0:T(8,128)(2,1)}, f32[8,128]{1,0:T(8,128)}) custom-call(f32[8,512]{1,0:T(8,128)} %user_ref.3, bf16[512,512]{1,0:T(8,128)(2,1)} %item_ref.1, bf16[46,512]{1,0:T(8,128)(2,1)} %day_ref.3), custom_call_target="tpu_custom_call" | custom-call | tf_op jit(solution)/shard_map/gather_users/pallas_call | solution.py:136
  35.0 0.0 copy-start
  35.0 2.2 %copy-done = bf16[128,128,128]{2,1,0:T(8,128)(2,1)S(1)} copy-done((bf16[128,128,128]{2,1,0:T(8,128)(2,1)S(1)}, bf16[128,128,128]{2,1,0:T(8,128)(2,1)}, u32[]{:S(2)}) %copy-start) | copy-done | bytes 4194328
  37.2 0.0 copy-start.1
  37.2 1.0 %copy-done.1 = bf16[512,512]{1,0:T(8,128)(2,1)S(1)} copy-done((bf16[512,512]{1,0:T(8,128)(2,1)S(1)}, bf16[512,512]{1,0:T(8,128)(2,1)}, u32[]{:S(2)}) %copy-start.1) | copy-done | bytes 524312
  38.2 0.0 copy-start.2
  38.2 1.6 %copy-done.2 = bf16[2,4,4,8,8,512]{5,4,3,2,1,0:T(8,128)(2,1)S(1)} copy-done((bf16[2,4,4,8,8,512]{5,4,3,2,1,0:T(8,128)(2,1)S(1)}, bf16[2,4,4,8,8,512]{5,4,3,2,1,0:T(8,128)(2,1)}, u32[]{:S(2)}) %copy-start.2) | copy-done | bytes 2097176
  39.8 0.0 copy-start.3
  39.8 0.8 copy-done.3
  40.6 0.0 copy-start.6
  40.6 0.7 copy-done.6
  41.3 0.0 copy-start.4
  41.3 0.0 copy-start.5
  41.3 9.4 %tile_turns.1 = f32[16,128,512]{2,1,0:T(8,128)S(1)} custom-call(s32[3,128]{1,0:T(4,128)S(1)} %copy-done.6, s32[1]{0:T(128)S(6)} %copy.8.live_ref, bf16[2,4,4,8,8,512]{5,4,3,2,1,0:T(8,128)(2,1)S(1)} %copy-done.2, bf16[4,128,512]{2,1,0:T(8,128)(2,1)S(1)} %bitcast.3, bf16[46,512]{1,0:T(8,128)(2,1)S(1)} %copy-done.3, bf16[128,128,128]{2,1,0:T(8,128)(2,1)S(1)} %copy-done), custom_call_target="tpu_custom_call" | custom-call | tf_op jit(solution)/shard_map/tile_turns/pallas_call | solution.py:260
  50.7 0.0 copy-done.4
  50.7 0.0 copy-done.5
  50.7 32.0 %sum_phi.1 = f32[8,512]{1,0:T(8,128)S(1)} custom-call(f32[4,8,4,2,8,512]{5,4,3,2,1,0:T(8,128)S(1)} %bitcast.2, f32[8,512]{1,0:T(8,128)S(1)} %copy-done.4, f32[8,128]{1,0:T(8,128)S(1)} %copy-done.5), custom_call_target="tpu_custom_call" | custom-call | tf_op jit(solution)/shard_map/sum_phi/pallas_call | solution.py:349
  82.7 0.6 copy.9
Async XLA Ops:
  35.0 2.2 %copy-start = (bf16[128,128,128]{2,1,0:T(8,128)(2,1)S(1)}, bf16[128,128,128]{2,1,0:T(8,128)(2,1)}, u32[]{:S(2)}) copy-start(bf16[128,128,128]{2,1,0:T(8,128)(2,1)} %counts_ref.1) | copy-start | bytes 12582916
  37.2 1.0 %copy-start.1 = (bf16[512,512]{1,0:T(8,128)(2,1)S(1)}, bf16[512,512]{1,0:T(8,128)(2,1)}, u32[]{:S(2)}) copy-start(bf16[512,512]{1,0:T(8,128)(2,1)} %item_ref.1) | copy-start | bytes 1572868
  38.2 1.6 %copy-start.2 = (bf16[2,4,4,8,8,512]{5,4,3,2,1,0:T(8,128)(2,1)S(1)}, bf16[2,4,4,8,8,512]{5,4,3,2,1,0:T(8,128)(2,1)}, u32[]{:S(2)}) copy-start(bf16[2,4,4,8,8,512]{5,4,3,2,1,0:T(8,128)(2,1)} %get-tuple-element.7.all_ref) | copy-start | bytes 6291460
  39.8 0.8 copy-start.3
  40.6 0.7 copy-start.6
  41.3 9.4 %copy-start.4 = (f32[8,512]{1,0:T(8,128)S(1)}, f32[8,512]{1,0:T(8,128)}, u32[]{:S(2)}) copy-start(f32[8,512]{1,0:T(8,128)} %user_ref.3) | copy-start | bytes 49156
  41.3 9.4 %copy-start.5 = (f32[8,128]{1,0:T(8,128)S(1)}, f32[8,128]{1,0:T(8,128)}, u32[]{:S(2)}) copy-start(f32[8,128]{1,0:T(8,128)} %get-tuple-element.8.total_ref) | copy-start | bytes 12292

commit v2 on v1

v2 whole, which is shorter than its diff:
```python
import functools

import jax
import jax.numpy as jnp
from jax import lax
from jax.experimental import pallas as pl
from jax.experimental.pallas import tpu as pltpu
from jax.sharding import PartitionSpec as P

MESH = pl.DeviceIdType.MESH
R = 512
TILE = 128
CAP = 128
USER_BLOCKS = 16
DAY_DEV = 46
ITEMBLK_DEV = 4
NX, NY, NZ, NC = 4, 4, 8, 2
ROWS = 8
FOUR = 4
KEEP = 96
DAY_ROWS = 48


def place():
    item, day = lax.axis_index("item"), lax.axis_index("day")
    x, z = lax.div(item, NZ), lax.rem(item, NZ)
    y, c = lax.div(day, NC), lax.rem(day, NC)
    return x, y, z, c


def device(x, y, z, c):
    return (x * NZ + z, y * NC + c)


def pick(c, zero, one):
    return zero + c * (one - zero)


def along(first, me, step):
    x, y, z, c = me
    return device(
        pick(first, lax.rem(x + step, NX), x), pick(first, y, lax.rem(y + step, NY)), z, c
    )


def greet(me):
    x, y, z, c = me
    barrier = pltpu.get_barrier_semaphore()
    for step in range(1, NZ):
        pl.semaphore_signal(
            barrier, inc=1, device_id=device(x, y, lax.rem(z + step, NZ), c), device_id_type=MESH
        )
    for step in range(1, NX):
        for first in (0, 1):
            pl.semaphore_signal(
                barrier, inc=1, device_id=along(first, me, step), device_id_type=MESH
            )
    pl.semaphore_signal(barrier, inc=1, device_id=device(x, y, z, 1 - c), device_id_type=MESH)


def welcome():
    pl.semaphore_wait(pltpu.get_barrier_semaphore(), NZ - 1 + 2 * (NX - 1) + 1)


def send(src, dst, sems, spot, target):
    copy = pltpu.make_async_remote_copy(
        src_ref=src,
        dst_ref=dst,
        send_sem=sems[0].at[spot],
        recv_sem=sems[1].at[spot],
        device_id=target,
        device_id_type=MESH,
    )
    copy.start()
    return copy


def order_slots(mine, theirs):
    lane = lax.broadcasted_iota(jnp.int32, (1, CAP), 1)
    own = lane < KEEP
    users, items, days, live = (
        jnp.where(own, mine[row : row + 1], theirs[row : row + 1]) for row in range(4)
    )
    days = jnp.where(own, days, days + DAY_ROWS)
    code = 1 + lane + 128 * users + 2048 * items + 8192 * days
    users = jnp.where(lane < live, users, USER_BLOCKS)
    first = lax.broadcasted_iota(jnp.int32, (CAP, CAP), 0)
    second = lax.broadcasted_iota(jnp.int32, (CAP, CAP), 1)

    def column(row):
        return jnp.sum(jnp.where(first == second, row, 0), axis=1, keepdims=True)

    same = (column(users) == users) & (first < second)
    rank = jnp.sum(same.astype(jnp.int32), axis=0, keepdims=True)
    block = lax.broadcasted_iota(jnp.int32, (USER_BLOCKS, CAP), 0)
    sizes = jnp.sum((block == users).astype(jnp.int32), axis=1, keepdims=True)
    padded = lax.shift_left(lax.shift_right_logical(sizes + (FOUR - 1), 2), 2)
    before = jnp.sum(jnp.where(block < users, padded, 0), axis=0, keepdims=True)
    spot = column(jnp.where(users < USER_BLOCKS, before + rank, 2 * CAP))
    codes = column(code)
    rows = [
        jnp.sum(jnp.where(spot == second + half * CAP, codes, 0), axis=0, keepdims=True)
        for half in (0, 1)
    ]
    groups = jnp.sum(lax.shift_right_logical(padded, 2), axis=0, keepdims=True)
    return rows[0], rows[1], jnp.broadcast_to(groups, (1, CAP))


def gather_kernel(
    user_hbm, item_hbm, day_hbm, counts_hbm, index_hbm, live_ref,
    users, items, days, counts, plan, total_ref,
    user_ref, day_ref, index_ref, meta, meta_in, sums, sums_c, sums_b, sums_a, sums_z,
    local_sem, z_s, z_r, a_s, a_r, b_s, b_r, c_s, c_r, m_s, m_r,
    tc_s, tc_r, tb_s, tb_r, ta_s, ta_r, tz_s, tz_r,
):
    me = place()
    x, y, z, c = me
    load_user, load_index, load_day, load_items, load_counts = (
        pltpu.make_async_copy(src, dst, local_sem.at[spot])
        for spot, (src, dst) in enumerate((
            (user_hbm, user_ref), (index_hbm, index_ref), (day_hbm, day_ref),
            (item_hbm, items), (counts_hbm.at[pl.ds(0, KEEP)], counts.at[pl.ds(0, KEEP)]),
        ))
    )
    for copy in (load_user, load_index, load_day, load_items, load_counts):
        copy.start()
    greet(me)
    load_user.wait()
    users[x, z, y, c] = user_ref[...].astype(jnp.bfloat16)
    welcome()
    other = device(x, y, z, 1 - c)

    spot = users.at[x, z, y, c]
    along_z = [
        send(spot, spot, (z_s, z_r), step - 1, device(x, y, lax.rem(z + step, NZ), c))
        for step in range(1, NZ)
    ]
    load_index.wait()
    load_day.wait()
    days[DAY_ROWS - 8 : DAY_ROWS, :] = jnp.zeros((8, R), jnp.float32)
    days[0:DAY_DEV, :] = day_ref[...].astype(jnp.float32)
    meta[...] = jnp.zeros_like(meta)
    meta[0:3, :] = index_ref[...]
    meta[3:4, :] = jnp.full((1, CAP), live_ref[0], jnp.int32)
    swapped = [
        send(meta, meta_in, (m_s, m_r), 0, other),
        send(days.at[pl.ds(0, DAY_ROWS)], days.at[pl.ds(DAY_ROWS, DAY_ROWS)], (m_s, m_r), 1, other),
        send(
            counts_hbm.at[pl.ds(KEEP, CAP - KEEP)], counts.at[pl.ds(KEEP, CAP - KEEP)],
            (m_s, m_r), 2, other,
        ),
    ]
    load_items.wait()
    item_sum = jnp.sum(items[...].astype(jnp.float32), axis=0, keepdims=True)
    day_sum = jnp.sum(day_ref[...].astype(jnp.float32), axis=0, keepdims=True)
    for part in range(R // 128):
        lanes = slice(part * 128, (part + 1) * 128)
        sums[part : part + 1, :] = item_sum[:, lanes]
        sums[part + 4 : part + 5, :] = day_sum[:, lanes]
    add = send(sums, sums_c, (tc_s, tc_r), 0, other)
    add.wait()
    sums[...] += sums_c[...]
    adds = [
        send(sums, sums_b.at[step - 1], (tb_s, tb_r), step - 1, along(1 - c, me, step))
        for step in range(1, NX)
    ]

    for copy in along_z:
        copy.wait()
    spot = users.at[x, :, y, c]
    along_a = [
        send(spot, spot, (a_s, a_r), step - 1, along(c, me, step)) for step in range(1, NX)
    ]
    for copy in adds:
        copy.wait()
    sums[...] += jnp.sum(sums_b[...], axis=0)
    adds = [
        send(sums, sums_a.at[step - 1], (ta_s, ta_r), step - 1, along(c, me, step))
        for step in range(1, NX)
    ]

    for copy in along_a:
        copy.wait()
    along_b = {}
    passed = []
    for part in range(NX):
        spot = users.at[pick(c, part, x), :, pick(c, y, part), c]
        for step in (1, 3, 2):
            along_b[part, step] = send(
                spot, spot, (b_s, b_r), (step - 1, part), along(1 - c, me, step)
            )
        passed.append(send(spot, spot, (c_s, c_r), (0, part), other))
    for copy in adds:
        copy.wait()
    sums[...] += jnp.sum(sums_a[...], axis=0)
    adds = [
        send(sums, sums_z.at[step - 1], (tz_s, tz_r), step - 1, device(x, y, lax.rem(z + step, NZ), c))
        for step in range(1, NZ)
    ]
    swapped[0].wait()
    first, second, groups = order_slots(meta[...], meta_in[...])
    plan[0:1, :] = first
    plan[1:2, :] = second
    plan[2:3, :] = groups
    plan[3:8, :] = jnp.zeros((5, CAP), jnp.int32)

    for part in range(NX):
        for step in (1, 3, 2):
            along_b[part, step].wait()
            x_from, y_from = lax.rem(x - step + NX, NX), lax.rem(y - step + NY, NY)
            spot = users.at[pick(c, part, x_from), :, pick(c, y_from, part), c]
            passed.append(send(spot, spot, (c_s, c_r), (step, part), other))
    for copy in adds:
        copy.wait()
    total_ref[...] = sums[...] + jnp.sum(sums_z[...], axis=0)
    swapped[1].wait()
    swapped[2].wait()
    load_counts.wait()
    for copy in passed:
        copy.wait()


def gather_call(user_factors, item_factors, day_factors, tile_counts, tile_index, tile_live):
    dma = pltpu.SemaphoreType.DMA
    vmem = pl.BlockSpec(memory_space=pltpu.VMEM)
    hbm = pl.BlockSpec(memory_space=pltpu.HBM)
    tile = (8, 128)
    return pl.pallas_call(
        gather_kernel,
        out_shape=(
            pltpu.VMEM((NX, NZ, NY, NC, ROWS, R), jnp.bfloat16),
            pltpu.VMEM((ITEMBLK_DEV * TILE, R), jnp.bfloat16),
            pltpu.VMEM((2 * DAY_ROWS, R), jnp.float32),
            pltpu.VMEM((CAP, TILE, TILE), jnp.bfloat16),
            pltpu.VMEM(tile, jnp.int32),
            pltpu.VMEM(tile, jnp.float32),
        ),
        in_specs=[hbm] * 5 + [pl.BlockSpec(memory_space=pltpu.SMEM)],
        out_specs=(vmem,) * 6,
        scratch_shapes=[
            pltpu.VMEM((ROWS, R), jnp.float32),
            pltpu.VMEM((DAY_DEV, R), jnp.bfloat16),
            pltpu.VMEM((3, CAP), jnp.int32),
            pltpu.VMEM(tile, jnp.int32),
            pltpu.VMEM(tile, jnp.int32),
            pltpu.VMEM(tile, jnp.float32),
            pltpu.VMEM(tile, jnp.float32),
            pltpu.VMEM((NX - 1,) + tile, jnp.float32),
            pltpu.VMEM((NX - 1,) + tile, jnp.float32),
            pltpu.VMEM((NZ - 1,) + tile, jnp.float32),
            dma((5,)),
        ]
        + [dma((NZ - 1,))] * 2 + [dma((NX - 1,))] * 2 + [dma((NX - 1, NX))] * 2
        + [dma((NX, NX))] * 2 + [dma((3,))] * 2
        + [dma((1,))] * 2 + [dma((NX - 1,))] * 4 + [dma((NZ - 1,))] * 2,
        compiler_params=pltpu.CompilerParams(
            collective_id=0, has_side_effects=True, vmem_limit_bytes=8 << 20
        ),
        name="gather_users",
    )(user_factors, item_factors, day_factors, tile_counts, tile_index, tile_live)


def phi_kernel(
    plan_ref, users_ref, item_ref, day_ref, counts_ref, phi_ref, w_even, w_odd, m_even, m_odd
):
    phi_ref[...] = jnp.zeros_like(phi_ref)
    groups = plan_ref[2, 0]

    def codes(group):
        spot = FOUR * group
        row, col = lax.shift_right_logical(spot, 7), spot & (CAP - 1)
        return [plan_ref[row, col + part] for part in range(FOUR)]

    def user_block(code):
        return lax.shift_right_logical(jnp.maximum(code - 1, 0), 7) & (USER_BLOCKS - 1)

    def forward(group, w, m):
        group_codes = codes(group)
        for part, code in enumerate(group_codes):
            code = jnp.maximum(code - 1, 0)
            items = item_ref[lax.shift_right_logical(code, 11) & 3]
            scale = day_ref[pl.ds(lax.shift_right_logical(code, 13), 1), :]
            scale = jnp.broadcast_to(scale, (16, R)).astype(jnp.bfloat16)
            scaled = items.reshape(TILE // 16, 16, R) * scale[None]
            w[part * TILE : (part + 1) * TILE, :] = scaled.reshape(TILE, R)
        m[...] = lax.dot_general(
            users_ref[user_block(group_codes[0])], w[...], (((1,), (1,)), ((), ())),
            preferred_element_type=jnp.float32,
        )

    def backward(group, w, m):
        group_codes = codes(group)
        ratios = []
        for part, code in enumerate(group_codes):
            tile = counts_ref[jnp.maximum(code - 1, 0) & (CAP - 1)].astype(jnp.float32)
            ratio = tile / m[:, part * TILE : (part + 1) * TILE]
            ratios.append(jnp.where(code > 0, ratio, 0.0).astype(jnp.bfloat16))
        phi_ref[user_block(group_codes[0])] += jnp.dot(
            jnp.concatenate(ratios, axis=1), w[...], preferred_element_type=jnp.float32
        )

    forward(0, w_even, m_even)

    def turn(pair, carry):
        group = 2 * pair
        forward(group + 1, w_odd, m_odd)
        backward(group, w_even, m_even)
        forward(group + 2, w_even, m_even)
        backward(group + 1, w_odd, m_odd)
        return carry

    lax.fori_loop(0, lax.shift_right_logical(groups + 1, 1), turn, 0)


def phi_call(plan, users, items, days, counts):
    vmem = pl.BlockSpec(memory_space=pltpu.VMEM)
    w = pltpu.VMEM((FOUR * TILE, R), jnp.bfloat16)
    m = pltpu.VMEM((TILE, FOUR * TILE), jnp.float32)
    return pl.pallas_call(
        phi_kernel,
        out_shape=pltpu.VMEM((USER_BLOCKS, TILE, R), jnp.float32),
        in_specs=[pl.BlockSpec(memory_space=pltpu.SMEM)] + [vmem] * 4,
        out_specs=vmem,
        scratch_shapes=[w, w, m, m],
        compiler_params=pltpu.CompilerParams(vmem_limit_bytes=32 << 20),
        name="tile_turns",
    )(plan, users, items, days, counts)


def scatter_kernel(
    phi_ref, user_ref, total_ref, out_ref,
    other, out_near, near, kept, far, deep,
    o_s, o_r, n_s, n_r, f_s, f_r, d_s, d_r,
):
    me = place()
    x, y, z, c = me
    p, q = pick(c, y, x), pick(c, x, y)
    greet(me)
    welcome()
    sibling = device(x, y, z, 1 - c)
    pairs = [(kp, kq) for kq in (1, 2, 3, 0) for kp in (1, 2, 3, 0)]
    crossed = {}
    for kp, kq in pairs:
        pp, qq = lax.rem(q + kp, NX), lax.rem(p + kq, NX)
        src = phi_ref.at[pick(c, pp, qq), :, pick(c, qq, pp), 1 - c]
        crossed[kp, kq] = send(src, other.at[kp, kq], (o_s, o_r), (kp, kq), sibling)

    nears, fars = {}, {}
    for kp, kq in pairs:
        pp, qq = lax.rem(p + kp, NX), lax.rem(q + kq, NX)
        crossed[kp, kq].wait()
        piece = phi_ref[pick(c, qq, pp), :, pick(c, pp, qq), c] + other[kp, kq]
        if kp:
            out_near[kp - 1, kq] = piece.reshape(NZ * ROWS, R).astype(jnp.bfloat16)
            nears[kp, kq] = send(
                out_near.at[kp - 1, kq], near.at[kp - 1, kq], (n_s, n_r), (kp - 1, kq),
                along(1 - c, me, kp),
            )
        else:
            kept[kq] = piece
    for kq in (1, 2, 3, 0):
        piece = kept[kq]
        for kp in (1, 2, 3):
            nears[kp, kq].wait()
            piece += near[kp - 1, kq].astype(jnp.float32).reshape(NZ, ROWS, R)
        kept[kq] = piece
        if kq:
            fars[kq] = send(kept.at[kq], far.at[kq - 1], (f_s, f_r), kq - 1, along(c, me, kq))
    for kq in (1, 2, 3):
        fars[kq].wait()
    kept[0] += far[0] + far[1] + far[2]
    deeps = []
    for step in range(1, NZ):
        there = lax.rem(z + step, NZ)
        deeps.append(
            send(kept.at[0, there], deep.at[step - 1], (d_s, d_r), step - 1,
                 device(x, y, there, c))
        )
    totals = total_ref[0:4, :] * total_ref[4:8, :] * (1.0 / (NX * NZ * NY * NC))
    for copy in deeps:
        copy.wait()
    summed = kept[0, z] + jnp.sum(deep[...], axis=0)
    for part in range(R // 128):
        lanes = slice(part * 128, (part + 1) * 128)
        out_ref[:, lanes] = user_ref[:, lanes] * summed[:, lanes] / totals[part : part + 1, :]


def scatter_call(phi, user_factors, totals):
    dma = pltpu.SemaphoreType.DMA
    vmem = pl.BlockSpec(memory_space=pltpu.VMEM)
    piece = (NZ, ROWS, R)
    return pl.pallas_call(
        scatter_kernel,
        out_shape=jax.ShapeDtypeStruct((ROWS, R), jnp.float32),
        in_specs=[vmem] * 3,
        out_specs=vmem,
        scratch_shapes=[
            pltpu.VMEM((NX, NX) + piece, jnp.float32),
            pltpu.VMEM((NX - 1, NX, NZ * ROWS, R), jnp.bfloat16),
            pltpu.VMEM((NX - 1, NX, NZ * ROWS, R), jnp.bfloat16),
            pltpu.VMEM((NX,) + piece, jnp.float32),
            pltpu.VMEM((NX - 1,) + piece, jnp.float32),
            pltpu.VMEM((NZ - 1, ROWS, R), jnp.float32),
            dma((NX, NX)), dma((NX, NX)),
            dma((NX - 1, NX)), dma((NX - 1, NX)),
            dma((NX - 1,)), dma((NX - 1,)),
            dma((NZ - 1,)), dma((NZ - 1,)),
        ],
        compiler_params=pltpu.CompilerParams(
            collective_id=1, has_side_effects=True, vmem_limit_bytes=24 << 20
        ),
        name="sum_phi",
    )(phi, user_factors, totals)


def per_device(user_factors, item_factors, day_factors, tile_counts, tile_index, tile_live):
    in_hbm = functools.partial(pltpu.with_memory_space_constraint, memory_space=pltpu.HBM)
    users, items, days, counts, plan, totals = gather_call(
        *map(in_hbm, (user_factors, item_factors, day_factors, tile_counts, tile_index)), tile_live
    )
    phi = phi_call(
        plan, users.reshape(USER_BLOCKS, TILE, R), items.reshape(ITEMBLK_DEV, TILE, R), days, counts
    )
    return scatter_call(phi.reshape(NX, NZ, NY, NC, ROWS, R), user_factors, totals)


def solution(mesh):
    in_specs = (
        P(("item", "day"), None),
        P("item", None),
        P("day", None),
        P(("item", "day"), None, None),
        P(None, ("item", "day")),
        P(("item", "day")),
    )
    out_specs = P(("item", "day"), None)
    return jax.shard_map(
        per_device, mesh=mesh, in_specs=in_specs, out_specs=out_specs, check_vma=False
    )
```

time: 84.9 us -> 63.8 us (0.75); the launches traced: 83.3 us -> 63.7 us
  Pallas kernels: 75.7 us -> 62.4 us
  local copies, waits for them, and re-layouts: 6.91 us -> 0.61 us
    pallas_call x2, Pallas kernels: 43.7 us -> 35.5 us  [the longest x1 28.8 us: gather_call(): pl.pallas_call(gather_kernel, out_shape=(pltpu.VMEM((NX, NZ, NY, NC, ROWS...]
    unnamed x15 -> x3, local copies, waits for them, and re-layouts: 6.91 us -> 0.61 us
    pallas_call x1, Pallas kernels: 32 us -> 26.9 us  [scatter_call(): pl.pallas_call(scatter_kernel, out_shape=jax.ShapeDtypeStruct((ROWS, R),...]
where the time goes in v2:
time: 63.8 us; the launch traced here: 63.7 us
  Pallas kernels  62.4 us (98%)
  between operations  0.69 us (1%)
    pallas_call x1, Pallas kernels, gather_call(): pl.pallas_call(gather_kernel, out_shape=(pltpu.VMEM((NX, NZ, NY, NC, ROWS...  28.8 us
    pallas_call x1, Pallas kernels, scatter_call(): pl.pallas_call(scatter_kernel, out_shape=jax.ShapeDtypeStruct((ROWS, R),...  26.9 us
    pallas_call x1, Pallas kernels, phi_call(): pl.pallas_call(phi_kernel, out_shape=pltpu.VMEM((USER_BLOCKS, TILE, R), j...  6.66 us

profile of v2, /device:TPU:6, one launch (start us, length us, event | category | flops | bytes accessed | tf_op | source)
XLA Modules:
  0.0 63.7 jit_solution(1413584691067559296)
XLA Ops:
  0.7 28.8 %gather_users.1 = (bf16[4,8,4,2,8,512]{5,4,3,2,1,0:T(8,128)(2,1)S(1)}, bf16[512,512]{1,0:T(8,128)(2,1)S(1)}, f32[96,512]{1,0:T(8,128)S(1)}, bf16[128,128,128]{2,...) custom-call(f32[8,512]{1,0:T(8,128)} %user_ref.1, bf16[512,512]{1,0:T(8,128)(2,1)} %item_hbm.1, ...), custom_call_target="tpu_custom_call" | custom-call | tf_op jit(solution)/shard_map/gather_users/pallas_call | solution.py:228
  29.5 0.0 copy-start
  29.5 6.7 %tile_turns.1 = f32[16,128,512]{2,1,0:T(8,128)S(1)} custom-call(s32[8,128]{1,0:T(8,128)S(1)} %get-tuple-element.11.plan_ref, bf16[16,128,512]{2,1,0:T(8,128)(2,1)S(1)} %bitcast.4, bf16[4,128,512]{2,1,0:T(8,128)(2,1)S(1)} %bitcast.5, f32[96,512]{1,0:T(8,128)S(1)} %get-tuple-element.14.day_ref, bf16[128,128,128]{2,1,0:T(8,128)(2,1)S(1)} %get-tuple-element.15.counts_ref), custom_call_target="tpu_custom_call" | custom-call | tf_op jit(solution)/shard_map/tile_turns/pallas_call | solution.py:319
  36.1 0.0 copy-done
  36.1 26.9 %sum_phi.1 = f32[8,512]{1,0:T(8,128)S(1)} custom-call(f32[4,8,4,2,8,512]{5,4,3,2,1,0:T(8,128)S(1)} %bitcast.3, f32[8,512]{1,0:T(8,128)S(1)} %copy-done, f32[8,128]{1,0:T(8,128)S(1)} %get-tuple-element.16.total_ref), custom_call_target="tpu_custom_call" | custom-call | tf_op jit(solution)/shard_map/sum_phi/pallas_call | solution.py:392
  63.1 0.6 copy.9
Async XLA Ops:
  29.5 6.7 %copy-start = (f32[8,512]{1,0:T(8,128)S(1)}, f32[8,512]{1,0:T(8,128)}, u32[]{:S(2)}) copy-start(f32[8,512]{1,0:T(8,128)} %user_ref.1) | copy-start | bytes 49156

commit v3 on v2

--- a/solution.py
+++ b/solution.py
@@ -19,6 +19,8 @@
 FOUR = 4
 KEEP = 96
 DAY_ROWS = 48
+STEPS = (2, 1, 3, 0)
+SHARES = (pl.ds(0, 5), pl.ds(5, 3))
 
 
 def place():
@@ -41,6 +43,10 @@
     return device(
         pick(first, lax.rem(x + step, NX), x), pick(first, y, lax.rem(y + step, NY)), z, c
     )
+
+
+def z_place(ahead):
+    return (0, 1, 3, 5, 7, 6, 4, 2)[ahead]
 
 
 def greet(me):
@@ -126,19 +132,48 @@
         copy.start()
     greet(me)
     load_user.wait()
-    users[x, z, y, c] = user_ref[...].astype(jnp.bfloat16)
+    users[x, 0, y, c] = user_ref[...].astype(jnp.bfloat16)
     welcome()
     other = device(x, y, z, 1 - c)
 
-    spot = users.at[x, z, y, c]
-    along_z = [
-        send(spot, spot, (z_s, z_r), step - 1, device(x, y, lax.rem(z + step, NZ), c))
-        for step in range(1, NZ)
-    ]
+    a, b = pick(c, x, y), pick(c, y, x)
+
+    def piece(back_a, back_b, share):
+        a_from, b_from = lax.rem(a - back_a + NX, NX), lax.rem(b - back_b + NX, NX)
+        return users.at[pick(c, a_from, b_from), SHARES[share], pick(c, b_from, a_from), c]
+
+    def forward(back_a, share):
+        spot = piece(back_a, 0, share)
+        for step in (2, 1, 3):
+            along_b[step, back_a, share] = send(
+                spot, spot, (b_s, b_r), (step - 1, back_a, share), along(1 - c, me, step)
+            )
+        cross(back_a, 0, share)
+
+    def cross(back_a, back_b, share):
+        spot = piece(back_a, back_b, share)
+        passed.append(send(spot, spot, (c_s, c_r), (back_a, back_b, share), other))
+
+    def spread(share):
+        spot = piece(0, 0, share)
+        for step in (2, 1, 3):
+            along_a[step, share] = send(
+                spot, spot, (a_s, a_r), (step - 1, share), along(c, me, step)
+            )
+        forward(0, share)
+
+    along_a, along_b, passed = {}, {}, []
+    along_z = {
+        step: send(
+            users.at[x, 0, y, c], users.at[x, z_place(NZ - step), y, c], (z_s, z_r), step - 1,
+            device(x, y, lax.rem(z + step, NZ), c),
+        )
+        for step in (2, 6, 1, 7, 4, 3, 5)
+    }
     load_index.wait()
     load_day.wait()
-    days[DAY_ROWS - 8 : DAY_ROWS, :] = jnp.zeros((8, R), jnp.float32)
     days[0:DAY_DEV, :] = day_ref[...].astype(jnp.float32)
+    days[DAY_DEV:DAY_ROWS, :] = jnp.zeros((DAY_ROWS - DAY_DEV, R), jnp.float32)
     meta[...] = jnp.zeros_like(meta)
     meta[0:3, :] = index_ref[...]
     meta[3:4, :] = jnp.full((1, CAP), live_ref[0], jnp.int32)
@@ -158,19 +193,19 @@
         sums[part : part + 1, :] = item_sum[:, lanes]
         sums[part + 4 : part + 5, :] = day_sum[:, lanes]
     add = send(sums, sums_c, (tc_s, tc_r), 0, other)
+
+    for step in (7, 1, 6, 2):
+        along_z[step].wait()
+    spread(0)
     add.wait()
     sums[...] += sums_c[...]
     adds = [
         send(sums, sums_b.at[step - 1], (tb_s, tb_r), step - 1, along(1 - c, me, step))
         for step in range(1, NX)
     ]
-
-    for copy in along_z:
-        copy.wait()
-    spot = users.at[x, :, y, c]
-    along_a = [
-        send(spot, spot, (a_s, a_r), step - 1, along(c, me, step)) for step in range(1, NX)
-    ]
+    for step in (5, 3, 4):
+        along_z[step].wait()
+    spread(1)
     for copy in adds:
         copy.wait()
     sums[...] += jnp.sum(sums_b[...], axis=0)
@@ -178,18 +213,10 @@
         send(sums, sums_a.at[step - 1], (ta_s, ta_r), step - 1, along(c, me, step))
         for step in range(1, NX)
     ]
-
-    for copy in along_a:
-        copy.wait()
-    along_b = {}
-    passed = []
-    for part in range(NX):
-        spot = users.at[pick(c, part, x), :, pick(c, y, part), c]
+    for share in (0, 1):
         for step in (1, 3, 2):
-            along_b[part, step] = send(
-                spot, spot, (b_s, b_r), (step - 1, part), along(1 - c, me, step)
-            )
-        passed.append(send(spot, spot, (c_s, c_r), (0, part), other))
+            along_a[step, share].wait()
+            forward(step, share)
     for copy in adds:
         copy.wait()
     sums[...] += jnp.sum(sums_a[...], axis=0)
@@ -202,14 +229,13 @@
     plan[0:1, :] = first
     plan[1:2, :] = second
     plan[2:3, :] = groups
-    plan[3:8, :] = jnp.zeros((5, CAP), jnp.int32)
-
-    for part in range(NX):
+    plan[3:4, :] = jnp.full((1, CAP), z, jnp.int32)
+    plan[4:8, :] = jnp.zeros((4, CAP), jnp.int32)
+
+    for back_a, share in ((0, 0), (0, 1), (1, 0), (3, 0), (2, 0), (1, 1), (3, 1), (2, 1)):
         for step in (1, 3, 2):
-            along_b[part, step].wait()
-            x_from, y_from = lax.rem(x - step + NX, NX), lax.rem(y - step + NY, NY)
-            spot = users.at[pick(c, part, x_from), :, pick(c, y_from, part), c]
-            passed.append(send(spot, spot, (c_s, c_r), (step, part), other))
+            along_b[step, back_a, share].wait()
+            cross(back_a, step, share)
     for copy in adds:
         copy.wait()
     total_ref[...] = sums[...] + jnp.sum(sums_z[...], axis=0)
@@ -250,8 +276,8 @@
             pltpu.VMEM((NZ - 1,) + tile, jnp.float32),
             dma((5,)),
         ]
-        + [dma((NZ - 1,))] * 2 + [dma((NX - 1,))] * 2 + [dma((NX - 1, NX))] * 2
-        + [dma((NX, NX))] * 2 + [dma((3,))] * 2
+        + [dma((NZ - 1,))] * 2 + [dma((NX - 1, 2))] * 2 + [dma((NX - 1, NX, 2))] * 2
+        + [dma((NX, NX, 2))] * 2 + [dma((3,))] * 2
         + [dma((1,))] * 2 + [dma((NX - 1,))] * 4 + [dma((NZ - 1,))] * 2,
         compiler_params=pltpu.CompilerParams(
             collective_id=0, has_side_effects=True, vmem_limit_bytes=8 << 20
@@ -264,7 +290,15 @@
     plan_ref, users_ref, item_ref, day_ref, counts_ref, phi_ref, w_even, w_odd, m_even, m_odd
 ):
     phi_ref[...] = jnp.zeros_like(phi_ref)
-    groups = plan_ref[2, 0]
+    groups, z = plan_ref[2, 0], plan_ref[3, 0]
+
+    def user_rows(block):
+        halves = []
+        for half in (0, 1):
+            ahead = (2 * (block & 3) + half - z) & (NZ - 1)
+            spot = jnp.where(ahead <= NZ // 2, jnp.maximum(2 * ahead - 1, 0), 2 * (NZ - ahead))
+            halves.append(users_ref[lax.shift_right_logical(block, 2) * NZ + spot])
+        return jnp.concatenate(halves, axis=0)
 
     def codes(group):
         spot = FOUR * group
@@ -284,7 +318,7 @@
             scaled = items.reshape(TILE // 16, 16, R) * scale[None]
             w[part * TILE : (part + 1) * TILE, :] = scaled.reshape(TILE, R)
         m[...] = lax.dot_general(
-            users_ref[user_block(group_codes[0])], w[...], (((1,), (1,)), ((), ())),
+            user_rows(user_block(group_codes[0])), w[...], (((1,), (1,)), ((), ())),
             preferred_element_type=jnp.float32,
         )
 
@@ -329,7 +363,7 @@
 
 def scatter_kernel(
     phi_ref, user_ref, total_ref, out_ref,
-    other, out_near, near, kept, far, deep,
+    other, out_near, near, kept, out_far, far, deep,
     o_s, o_r, n_s, n_r, f_s, f_r, d_s, d_r,
 ):
     me = place()
@@ -338,37 +372,44 @@
     greet(me)
     welcome()
     sibling = device(x, y, z, 1 - c)
-    pairs = [(kp, kq) for kq in (1, 2, 3, 0) for kp in (1, 2, 3, 0)]
-    crossed = {}
-    for kp, kq in pairs:
-        pp, qq = lax.rem(q + kp, NX), lax.rem(p + kq, NX)
-        src = phi_ref.at[pick(c, pp, qq), :, pick(c, qq, pp), 1 - c]
-        crossed[kp, kq] = send(src, other.at[kp, kq], (o_s, o_r), (kp, kq), sibling)
-
-    nears, fars = {}, {}
-    for kp, kq in pairs:
-        pp, qq = lax.rem(p + kp, NX), lax.rem(q + kq, NX)
-        crossed[kp, kq].wait()
-        piece = phi_ref[pick(c, qq, pp), :, pick(c, pp, qq), c] + other[kp, kq]
-        if kp:
-            out_near[kp - 1, kq] = piece.reshape(NZ * ROWS, R).astype(jnp.bfloat16)
-            nears[kp, kq] = send(
-                out_near.at[kp - 1, kq], near.at[kp - 1, kq], (n_s, n_r), (kp - 1, kq),
-                along(1 - c, me, kp),
-            )
+    crossed, nears, fars = {}, {}, {}
+
+    def cross(kq):
+        for kp in STEPS:
+            pp, qq = lax.rem(q + kp, NX), lax.rem(p + kq, NX)
+            src = phi_ref.at[pick(c, pp, qq), :, pick(c, qq, pp), 1 - c]
+            crossed[kp, kq] = send(src, other.at[kp, kq], (o_s, o_r), (kp, kq), sibling)
+
+    cross(STEPS[0])
+    for turn, kq in enumerate(STEPS):
+        if turn + 1 < NX:
+            cross(STEPS[turn + 1])
+        for kp in STEPS:
+            pp, qq = lax.rem(p + kp, NX), lax.rem(q + kq, NX)
+            crossed[kp, kq].wait_recv()
+            piece = phi_ref[pick(c, qq, pp), :, pick(c, pp, qq), c] + other[kp, kq]
+            if kp:
+                out_near[kp - 1, kq] = piece.reshape(NZ * ROWS, R).astype(jnp.bfloat16)
+                nears[kp, kq] = send(
+                    out_near.at[kp - 1, kq], near.at[kp - 1, kq], (n_s, n_r), (kp - 1, kq),
+                    along(1 - c, me, kp),
+                )
+            else:
+                kept[kq] = piece
+    for kq in STEPS:
+        piece = kept[kq]
+        for kp in (1, 3, 2):
+            nears[kp, kq].wait_recv()
+            piece += near[kp - 1, kq].astype(jnp.float32).reshape(NZ, ROWS, R)
+        if kq:
+            out_far[kq - 1] = piece.reshape(NZ * ROWS, R).astype(jnp.bfloat16)
+            fars[kq] = send(out_far.at[kq - 1], far.at[kq - 1], (f_s, f_r), kq - 1, along(c, me, kq))
         else:
-            kept[kq] = piece
-    for kq in (1, 2, 3, 0):
-        piece = kept[kq]
-        for kp in (1, 2, 3):
-            nears[kp, kq].wait()
-            piece += near[kp - 1, kq].astype(jnp.float32).reshape(NZ, ROWS, R)
-        kept[kq] = piece
-        if kq:
-            fars[kq] = send(kept.at[kq], far.at[kq - 1], (f_s, f_r), kq - 1, along(c, me, kq))
+            kept[0] = piece
     for kq in (1, 2, 3):
-        fars[kq].wait()
-    kept[0] += far[0] + far[1] + far[2]
+        fars[kq].wait_recv()
+    arrived = jnp.sum(far[...].astype(jnp.float32), axis=0)
+    kept[0] += arrived.reshape(NZ, ROWS, R)
     deeps = []
     for step in range(1, NZ):
         there = lax.rem(z + step, NZ)
@@ -378,11 +419,14 @@
         )
     totals = total_ref[0:4, :] * total_ref[4:8, :] * (1.0 / (NX * NZ * NY * NC))
     for copy in deeps:
-        copy.wait()
+        copy.wait_recv()
     summed = kept[0, z] + jnp.sum(deep[...], axis=0)
     for part in range(R // 128):
         lanes = slice(part * 128, (part + 1) * 128)
         out_ref[:, lanes] = user_ref[:, lanes] * summed[:, lanes] / totals[part : part + 1, :]
+    for group in (crossed.values(), nears.values(), fars.values(), deeps):
+        for copy in group:
+            copy.wait_send()
 
 
 def scatter_call(phi, user_factors, totals):
@@ -399,7 +443,8 @@
             pltpu.VMEM((NX - 1, NX, NZ * ROWS, R), jnp.bfloat16),
             pltpu.VMEM((NX - 1, NX, NZ * ROWS, R), jnp.bfloat16),
             pltpu.VMEM((NX,) + piece, jnp.float32),
-            pltpu.VMEM((NX - 1,) + piece, jnp.float32),
+            pltpu.VMEM((NX - 1, NZ * ROWS, R), jnp.bfloat16),
+            pltpu.VMEM((NX - 1, NZ * ROWS, R), jnp.bfloat16),
             pltpu.VMEM((NZ - 1, ROWS, R), jnp.float32),
             dma((NX, NX)), dma((NX, NX)),
             dma((NX - 1, NX)), dma((NX - 1, NX)),
@@ -419,7 +464,7 @@
         *map(in_hbm, (user_factors, item_factors, day_factors, tile_counts, tile_index)), tile_live
     )
     phi = phi_call(
-        plan, users.reshape(USER_BLOCKS, TILE, R), items.reshape(ITEMBLK_DEV, TILE, R), days, counts
+        plan, users.reshape(NX * NZ, TILE // 2, R), items.reshape(ITEMBLK_DEV, TILE, R), days, counts
     )
     return scatter_call(phi.reshape(NX, NZ, NY, NC, ROWS, R), user_factors, totals)
 

time: 63.8 us -> 59.1 us (0.926); the launches traced: 63.7 us -> 58 us
  Pallas kernels: 62.4 us -> 56.7 us
    pallas_call x1, Pallas kernels: 26.9 us -> 22.9 us  [scatter_call(): pl.pallas_call(scatter_kernel, out_shape=jax.ShapeDtypeStruct((ROWS, R),...]
    pallas_call x1, Pallas kernels: 28.8 us -> 26.4 us  [gather_call(): pl.pallas_call(gather_kernel, out_shape=(pltpu.VMEM((NX, NZ, NY, NC, ROWS...]
    pallas_call x1, Pallas kernels: 6.66 us -> 7.36 us  [phi_call(): pl.pallas_call(phi_kernel, out_shape=pltpu.VMEM((USER_BLOCKS, TILE, R), j...]
where the time goes in v3:
time: 59.1 us; the launch traced here: 58 us
  Pallas kernels  56.7 us (96%)
  between operations  0.69 us (1%)
  local copies, waits for them, and re-layouts  0.61 us (1%)
    pallas_call x1, Pallas kernels, gather_call(): pl.pallas_call(gather_kernel, out_shape=(pltpu.VMEM((NX, NZ, NY, NC, ROWS...  26.4 us
    pallas_call x1, Pallas kernels, scatter_call(): pl.pallas_call(scatter_kernel, out_shape=jax.ShapeDtypeStruct((ROWS, R),...  22.9 us
    pallas_call x1, Pallas kernels, phi_call(): pl.pallas_call(phi_kernel, out_shape=pltpu.VMEM((USER_BLOCKS, TILE, R), j...  7.36 us

profile of v3, /device:TPU:6, one launch (start us, length us, event | category | flops | bytes accessed | tf_op | source)
XLA Modules:
  0.0 58.0 jit_solution(12519611241099275828)
XLA Ops:
  0.7 26.4 %gather_users.1 = (bf16[4,8,4,2,8,512]{5,4,3,2,1,0:T(8,128)(2,1)S(1)}, bf16[512,512]{1,0:T(8,128)(2,1)S(1)}, f32[96,512]{1,0:T(8,128)S(1)}, bf16[128,128,128]{2,...) custom-call(f32[8,512]{1,0:T(8,128)} %user_ref.1, bf16[512,512]{1,0:T(8,128)(2,1)} %item_hbm.1, ...), custom_call_target="tpu_custom_call" | custom-call | tf_op jit(solution)/shard_map/gather_users/pallas_call | solution.py:254
  27.1 0.0 copy-start
  27.1 7.4 %tile_turns.1 = f32[16,128,512]{2,1,0:T(8,128)S(1)} custom-call(s32[8,128]{1,0:T(8,128)S(1)} %get-tuple-element.11.plan_ref, bf16[32,64,512]{2,1,0:T(8,128)(2,1)S(1)} %bitcast.4, bf16[4,128,512]{2,1,0:T(8,128)(2,1)S(1)} %bitcast.5, f32[96,512]{1,0:T(8,128)S(1)} %get-tuple-element.14.day_ref, bf16[128,128,128]{2,1,0:T(8,128)(2,1)S(1)} %get-tuple-element.15.counts_ref), custom_call_target="tpu_custom_call" | custom-call | tf_op jit(solution)/shard_map/tile_turns/pallas_call | solution.py:353
  34.4 0.0 copy-done
  34.4 22.9 %sum_phi.1 = f32[8,512]{1,0:T(8,128)S(1)} custom-call(f32[4,8,4,2,8,512]{5,4,3,2,1,0:T(8,128)S(1)} %bitcast.3, f32[8,512]{1,0:T(8,128)S(1)} %copy-done, f32[8,128]{1,0:T(8,128)S(1)} %get-tuple-element.16.total_ref), custom_call_target="tpu_custom_call" | custom-call | tf_op jit(solution)/shard_map/sum_phi/pallas_call | solution.py:436
  57.4 0.6 %copy.9 = f32[8,512]{1,0:T(8,128)} copy(f32[8,512]{1,0:T(8,128)S(1)} %sum_phi.1) | data formatting | bytes 32768
Async XLA Ops:
  27.1 7.4 %copy-start = (f32[8,512]{1,0:T(8,128)S(1)}, f32[8,512]{1,0:T(8,128)}, u32[]{:S(2)}) copy-start(f32[8,512]{1,0:T(8,128)} %user_ref.1) | copy-start | bytes 49156

commit v4 on v3

--- a/solution.py
+++ b/solution.py
@@ -17,7 +17,7 @@
 NX, NY, NZ, NC = 4, 4, 8, 2
 ROWS = 8
 FOUR = 4
-KEEP = 96
+KEEP = 64
 DAY_ROWS = 48
 STEPS = (2, 1, 3, 0)
 SHARES = (pl.ds(0, 5), pl.ds(5, 3))
@@ -83,33 +83,46 @@
 
 def order_slots(mine, theirs):
     lane = lax.broadcasted_iota(jnp.int32, (1, CAP), 1)
-    own = lane < KEEP
-    users, items, days, live = (
-        jnp.where(own, mine[row : row + 1], theirs[row : row + 1]) for row in range(4)
-    )
-    days = jnp.where(own, days, days + DAY_ROWS)
-    code = 1 + lane + 128 * users + 2048 * items + 8192 * days
-    users = jnp.where(lane < live, users, USER_BLOCKS)
-    first = lax.broadcasted_iota(jnp.int32, (CAP, CAP), 0)
-    second = lax.broadcasted_iota(jnp.int32, (CAP, CAP), 1)
+
+    def kept(live, other):
+        return jnp.minimum(live, jnp.maximum(KEEP, lax.shift_right_logical(live + other + 1, 1)))
+
+    live, other = mine[3:4], theirs[3:4]
+    own = lane < kept(live, other)
+    taken = (lane >= kept(other, live)) & (lane < other)
+    users = jnp.concatenate(
+        [jnp.where(own, mine[0:1], USER_BLOCKS), jnp.where(taken, theirs[0:1], USER_BLOCKS)], axis=1
+    )
+    rest = jnp.concatenate(
+        [
+            1 + lane + 256 * mine[0:1] + 4096 * mine[1:2] + 16384 * mine[2:3],
+            1 + lane + KEEP + 256 * theirs[0:1] + 4096 * theirs[1:2] + 16384 * (theirs[2:3] + DAY_ROWS),
+        ],
+        axis=1,
+    )
+    first = lax.broadcasted_iota(jnp.int32, (2 * CAP, 2 * CAP), 0)
+    second = lax.broadcasted_iota(jnp.int32, (2 * CAP, 2 * CAP), 1)
 
     def column(row):
         return jnp.sum(jnp.where(first == second, row, 0), axis=1, keepdims=True)
 
     same = (column(users) == users) & (first < second)
     rank = jnp.sum(same.astype(jnp.int32), axis=0, keepdims=True)
-    block = lax.broadcasted_iota(jnp.int32, (USER_BLOCKS, CAP), 0)
+    block = lax.broadcasted_iota(jnp.int32, (USER_BLOCKS, 2 * CAP), 0)
     sizes = jnp.sum((block == users).astype(jnp.int32), axis=1, keepdims=True)
     padded = lax.shift_left(lax.shift_right_logical(sizes + (FOUR - 1), 2), 2)
     before = jnp.sum(jnp.where(block < users, padded, 0), axis=0, keepdims=True)
     spot = column(jnp.where(users < USER_BLOCKS, before + rank, 2 * CAP))
-    codes = column(code)
-    rows = [
-        jnp.sum(jnp.where(spot == second + half * CAP, codes, 0), axis=0, keepdims=True)
-        for half in (0, 1)
-    ]
+    codes = jnp.sum(jnp.where(spot == second, column(rest), 0), axis=0, keepdims=True)
     groups = jnp.sum(lax.shift_right_logical(padded, 2), axis=0, keepdims=True)
-    return rows[0], rows[1], jnp.broadcast_to(groups, (1, CAP))
+    return codes[:, :CAP], codes[:, CAP:], jnp.broadcast_to(groups, (1, CAP))
+
+
+def user_places(z):
+    lane = lax.broadcasted_iota(jnp.int32, (1, CAP), 1)
+    ahead = ((lane & 7) - z) & (NZ - 1)
+    spot = jnp.where(ahead <= NZ // 2, jnp.maximum(2 * ahead - 1, 0), 2 * (NZ - ahead))
+    return (lane - (lane & 7)) + spot
 
 
 def gather_kernel(
@@ -125,7 +138,7 @@
         pltpu.make_async_copy(src, dst, local_sem.at[spot])
         for spot, (src, dst) in enumerate((
             (user_hbm, user_ref), (index_hbm, index_ref), (day_hbm, day_ref),
-            (item_hbm, items), (counts_hbm.at[pl.ds(0, KEEP)], counts.at[pl.ds(0, KEEP)]),
+            (item_hbm, items), (counts_hbm, counts.at[pl.ds(0, CAP)]),
         ))
     )
     for copy in (load_user, load_index, load_day, load_items, load_counts):
@@ -181,7 +194,7 @@
         send(meta, meta_in, (m_s, m_r), 0, other),
         send(days.at[pl.ds(0, DAY_ROWS)], days.at[pl.ds(DAY_ROWS, DAY_ROWS)], (m_s, m_r), 1, other),
         send(
-            counts_hbm.at[pl.ds(KEEP, CAP - KEEP)], counts.at[pl.ds(KEEP, CAP - KEEP)],
+            counts_hbm.at[pl.ds(KEEP, CAP - KEEP)], counts.at[pl.ds(CAP, CAP - KEEP)],
             (m_s, m_r), 2, other,
         ),
     ]
@@ -229,7 +242,7 @@
     plan[0:1, :] = first
     plan[1:2, :] = second
     plan[2:3, :] = groups
-    plan[3:4, :] = jnp.full((1, CAP), z, jnp.int32)
+    plan[3:4, :] = user_places(z)
     plan[4:8, :] = jnp.zeros((4, CAP), jnp.int32)
 
     for back_a, share in ((0, 0), (0, 1), (1, 0), (3, 0), (2, 0), (1, 1), (3, 1), (2, 1)):
@@ -257,7 +270,7 @@
             pltpu.VMEM((NX, NZ, NY, NC, ROWS, R), jnp.bfloat16),
             pltpu.VMEM((ITEMBLK_DEV * TILE, R), jnp.bfloat16),
             pltpu.VMEM((2 * DAY_ROWS, R), jnp.float32),
-            pltpu.VMEM((CAP, TILE, TILE), jnp.bfloat16),
+            pltpu.VMEM((2 * CAP - KEEP, TILE, TILE), jnp.bfloat16),
             pltpu.VMEM(tile, jnp.int32),
             pltpu.VMEM(tile, jnp.float32),
         ),
@@ -290,15 +303,10 @@
     plan_ref, users_ref, item_ref, day_ref, counts_ref, phi_ref, w_even, w_odd, m_even, m_odd
 ):
     phi_ref[...] = jnp.zeros_like(phi_ref)
-    groups, z = plan_ref[2, 0], plan_ref[3, 0]
+    groups = plan_ref[2, 0]
 
     def user_rows(block):
-        halves = []
-        for half in (0, 1):
-            ahead = (2 * (block & 3) + half - z) & (NZ - 1)
-            spot = jnp.where(ahead <= NZ // 2, jnp.maximum(2 * ahead - 1, 0), 2 * (NZ - ahead))
-            halves.append(users_ref[lax.shift_right_logical(block, 2) * NZ + spot])
-        return jnp.concatenate(halves, axis=0)
+        return jnp.concatenate([users_ref[plan_ref[3, 2 * block + half]] for half in (0, 1)], axis=0)
 
     def codes(group):
         spot = FOUR * group
@@ -306,14 +314,14 @@
         return [plan_ref[row, col + part] for part in range(FOUR)]
 
     def user_block(code):
-        return lax.shift_right_logical(jnp.maximum(code - 1, 0), 7) & (USER_BLOCKS - 1)
+        return lax.shift_right_logical(jnp.maximum(code - 1, 0), 8) & (USER_BLOCKS - 1)
 
     def forward(group, w, m):
         group_codes = codes(group)
         for part, code in enumerate(group_codes):
             code = jnp.maximum(code - 1, 0)
-            items = item_ref[lax.shift_right_logical(code, 11) & 3]
-            scale = day_ref[pl.ds(lax.shift_right_logical(code, 13), 1), :]
+            items = item_ref[lax.shift_right_logical(code, 12) & 3]
+            scale = day_ref[pl.ds(lax.shift_right_logical(code, 14), 1), :]
             scale = jnp.broadcast_to(scale, (16, R)).astype(jnp.bfloat16)
             scaled = items.reshape(TILE // 16, 16, R) * scale[None]
             w[part * TILE : (part + 1) * TILE, :] = scaled.reshape(TILE, R)
@@ -326,7 +334,7 @@
         group_codes = codes(group)
         ratios = []
         for part, code in enumerate(group_codes):
-            tile = counts_ref[jnp.maximum(code - 1, 0) & (CAP - 1)].astype(jnp.float32)
+            tile = counts_ref[jnp.maximum(code - 1, 0) & 255].astype(jnp.float32)
             ratio = tile / m[:, part * TILE : (part + 1) * TILE]
             ratios.append(jnp.where(code > 0, ratio, 0.0).astype(jnp.bfloat16))
         phi_ref[user_block(group_codes[0])] += jnp.dot(

time: 59.1 us -> 59.6 us (level); the launches traced: 58 us -> 59.5 us
  Pallas kernels: 56.7 us -> 58.2 us
    pallas_call x1, Pallas kernels: 22.9 us -> 24.4 us  [scatter_call(): pl.pallas_call(scatter_kernel, out_shape=jax.ShapeDtypeStruct((ROWS, R),...]
where the time goes in v4:
time: 59.6 us; the launch traced here: 59.5 us
  Pallas kernels  58.2 us (98%)
  between operations  0.69 us (1%)
  local copies, waits for them, and re-layouts  0.61 us (1%)
    pallas_call x1, Pallas kernels, gather_call(): pl.pallas_call(gather_kernel, out_shape=(pltpu.VMEM((NX, NZ, NY, NC, ROWS...  26.4 us
    pallas_call x1, Pallas kernels, scatter_call(): pl.pallas_call(scatter_kernel, out_shape=jax.ShapeDtypeStruct((ROWS, R),...  24.4 us
    pallas_call x1, Pallas kernels, phi_call(): pl.pallas_call(phi_kernel, out_shape=pltpu.VMEM((USER_BLOCKS, TILE, R), j...  7.35 us

profile of v4, /device:TPU:6, one launch (start us, length us, event | category | flops | bytes accessed | tf_op | source)
XLA Modules:
  0.0 59.5 jit_solution(2275356182118685615)
XLA Ops:
  0.7 26.4 %gather_users.1 = (bf16[4,8,4,2,8,512]{5,4,3,2,1,0:T(8,128)(2,1)S(1)}, bf16[512,512]{1,0:T(8,128)(2,1)S(1)}, f32[96,512]{1,0:T(8,128)S(1)}, bf16[192,128,128]{2,...) custom-call(f32[8,512]{1,0:T(8,128)} %user_ref.1, bf16[512,512]{1,0:T(8,128)(2,1)} %item_hbm.1, ...), custom_call_target="tpu_custom_call" | custom-call | tf_op jit(solution)/shard_map/gather_users/pallas_call | solution.py:267
  27.1 0.0 copy-start
  27.1 7.3 %tile_turns.1 = f32[16,128,512]{2,1,0:T(8,128)S(1)} custom-call(s32[8,128]{1,0:T(8,128)S(1)} %get-tuple-element.11.plan_ref, bf16[32,64,512]{2,1,0:T(8,128)(2,1)S(1)} %bitcast.4, bf16[4,128,512]{2,1,0:T(8,128)(2,1)S(1)} %bitcast.5, f32[96,512]{1,0:T(8,128)S(1)} %get-tuple-element.14.day_ref, bf16[192,128,128]{2,1,0:T(8,128)(2,1)S(1)} %get-tuple-element.15.counts_ref), custom_call_target="tpu_custom_call" | custom-call | tf_op jit(solution)/shard_map/tile_turns/pallas_call | solution.py:361
  34.4 0.0 copy-done
  34.4 24.4 %sum_phi.1 = f32[8,512]{1,0:T(8,128)S(1)} custom-call(f32[4,8,4,2,8,512]{5,4,3,2,1,0:T(8,128)S(1)} %bitcast.3, f32[8,512]{1,0:T(8,128)S(1)} %copy-done, f32[8,128]{1,0:T(8,128)S(1)} %get-tuple-element.16.total_ref), custom_call_target="tpu_custom_call" | custom-call | tf_op jit(solution)/shard_map/sum_phi/pallas_call | solution.py:444
  58.9 0.6 %copy.9 = f32[8,512]{1,0:T(8,128)} copy(f32[8,512]{1,0:T(8,128)S(1)} %sum_phi.1) | data formatting | bytes 32768
Async XLA Ops:
  27.1 7.4 %copy-start = (f32[8,512]{1,0:T(8,128)S(1)}, f32[8,512]{1,0:T(8,128)}, u32[]{:S(2)}) copy-start(f32[8,512]{1,0:T(8,128)} %user_ref.1) | copy-start | bytes 49156

commit v5 on v4

--- a/solution.py
+++ b/solution.py
@@ -52,7 +52,7 @@
 def greet(me):
     x, y, z, c = me
     barrier = pltpu.get_barrier_semaphore()
-    for step in range(1, NZ):
+    for step in (4, 3, 5, 2, 6, 1, 7):
         pl.semaphore_signal(
             barrier, inc=1, device_id=device(x, y, lax.rem(z + step, NZ), c), device_id_type=MESH
         )
@@ -127,8 +127,8 @@
 
 def gather_kernel(
     user_hbm, item_hbm, day_hbm, counts_hbm, index_hbm, live_ref,
-    users, items, days, counts, plan, total_ref,
-    user_ref, day_ref, index_ref, meta, meta_in, sums, sums_c, sums_b, sums_a, sums_z,
+    users, items, days, counts, plan_smem, total_ref,
+    user_ref, day_ref, index_ref, plan, meta, meta_in, sums, sums_c, sums_b, sums_a, sums_z,
     local_sem, z_s, z_r, a_s, a_r, b_s, b_r, c_s, c_r, m_s, m_r,
     tc_s, tc_r, tb_s, tb_r, ta_s, ta_r, tz_s, tz_r,
 ):
@@ -235,7 +235,7 @@
     sums[...] += jnp.sum(sums_a[...], axis=0)
     adds = [
         send(sums, sums_z.at[step - 1], (tz_s, tz_r), step - 1, device(x, y, lax.rem(z + step, NZ), c))
-        for step in range(1, NZ)
+        for step in (4, 3, 5, 2, 6, 1, 7)
     ]
     swapped[0].wait()
     first, second, groups = order_slots(meta[...], meta_in[...])
@@ -244,6 +244,8 @@
     plan[2:3, :] = groups
     plan[3:4, :] = user_places(z)
     plan[4:8, :] = jnp.zeros((4, CAP), jnp.int32)
+    hand_plan = pltpu.make_async_copy(plan, plan_smem, local_sem.at[5])
+    hand_plan.start()
 
     for back_a, share in ((0, 0), (0, 1), (1, 0), (3, 0), (2, 0), (1, 1), (3, 1), (2, 1)):
         for step in (1, 3, 2):
@@ -255,6 +257,7 @@
     swapped[1].wait()
     swapped[2].wait()
     load_counts.wait()
+    hand_plan.wait()
     for copy in passed:
         copy.wait()
 
@@ -271,15 +274,16 @@
             pltpu.VMEM((ITEMBLK_DEV * TILE, R), jnp.bfloat16),
             pltpu.VMEM((2 * DAY_ROWS, R), jnp.float32),
             pltpu.VMEM((2 * CAP - KEEP, TILE, TILE), jnp.bfloat16),
-            pltpu.VMEM(tile, jnp.int32),
+            pltpu.SMEM(tile, jnp.int32),
             pltpu.VMEM(tile, jnp.float32),
         ),
         in_specs=[hbm] * 5 + [pl.BlockSpec(memory_space=pltpu.SMEM)],
-        out_specs=(vmem,) * 6,
+        out_specs=(vmem,) * 4 + (pl.BlockSpec(memory_space=pltpu.SMEM), vmem),
         scratch_shapes=[
             pltpu.VMEM((ROWS, R), jnp.float32),
             pltpu.VMEM((DAY_DEV, R), jnp.bfloat16),
             pltpu.VMEM((3, CAP), jnp.int32),
+            pltpu.VMEM(tile, jnp.int32),
             pltpu.VMEM(tile, jnp.int32),
             pltpu.VMEM(tile, jnp.int32),
             pltpu.VMEM(tile, jnp.float32),
@@ -287,7 +291,7 @@
             pltpu.VMEM((NX - 1,) + tile, jnp.float32),
             pltpu.VMEM((NX - 1,) + tile, jnp.float32),
             pltpu.VMEM((NZ - 1,) + tile, jnp.float32),
-            dma((5,)),
+            dma((6,)),
         ]
         + [dma((NZ - 1,))] * 2 + [dma((NX - 1, 2))] * 2 + [dma((NX - 1, NX, 2))] * 2
         + [dma((NX, NX, 2))] * 2 + [dma((3,))] * 2
@@ -419,7 +423,7 @@
     arrived = jnp.sum(far[...].astype(jnp.float32), axis=0)
     kept[0] += arrived.reshape(NZ, ROWS, R)
     deeps = []
-    for step in range(1, NZ):
+    for step in (4, 3, 5, 2, 6, 1, 7):
         there = lax.rem(z + step, NZ)
         deeps.append(
             send(kept.at[0, there], deep.at[step - 1], (d_s, d_r), step - 1,

time: 59.6 us -> 58.6 us (0.983)
  Pallas kernels: 58.2 us -> 57.1 us
    pallas_call x1, Pallas kernels: 7.35 us -> 6.04 us  [phi_call(): pl.pallas_call(phi_kernel, out_shape=pltpu.VMEM((USER_BLOCKS, TILE, R), j...]
where the time goes in v5:
time: 58.6 us; the launch traced here: 58.4 us
  Pallas kernels  57.1 us (97%)
  between operations  0.69 us (1%)
  local copies, waits for them, and re-layouts  0.61 us (1%)
    pallas_call x1, Pallas kernels, gather_call(): pl.pallas_call(gather_kernel, out_shape=(pltpu.VMEM((NX, NZ, NY, NC, ROWS...  26.3 us
    pallas_call x1, Pallas kernels, scatter_call(): pl.pallas_call(scatter_kernel, out_shape=jax.ShapeDtypeStruct((ROWS, R),...  24.8 us
    pallas_call x1, Pallas kernels, phi_call(): pl.pallas_call(phi_kernel, out_shape=pltpu.VMEM((USER_BLOCKS, TILE, R), j...  6.04 us

profile of v5, /device:TPU:6, one launch (start us, length us, event | category | flops | bytes accessed | tf_op | source)
XLA Modules:
  0.0 58.4 jit_solution(7695346627482868843)
XLA Ops:
  0.7 26.3 %gather_users.1 = (bf16[4,8,4,2,8,512]{5,4,3,2,1,0:T(8,128)(2,1)S(1)}, bf16[512,512]{1,0:T(8,128)(2,1)S(1)}, f32[96,512]{1,0:T(8,128)S(1)}, bf16[192,128,128]{2,...) custom-call(f32[8,512]{1,0:T(8,128)} %user_ref.1, bf16[512,512]{1,0:T(8,128)(2,1)} %item_hbm.1, ...), custom_call_target="tpu_custom_call" | custom-call | tf_op jit(solution)/shard_map/gather_users/pallas_call | solution.py:270
  26.9 0.0 copy-start
  26.9 6.0 %tile_turns.1 = f32[16,128,512]{2,1,0:T(8,128)S(1)} custom-call(s32[8,128]{1,0:T(8,128)S(4)} %get-tuple-element.11.plan_ref, bf16[32,64,512]{2,1,0:T(8,128)(2,1)S(1)} %bitcast.4, bf16[4,128,512]{2,1,0:T(8,128)(2,1)S(1)} %bitcast.5, f32[96,512]{1,0:T(8,128)S(1)} %get-tuple-element.14.day_ref, bf16[192,128,128]{2,1,0:T(8,128)(2,1)S(1)} %get-tuple-element.15.counts_ref), custom_call_target="tpu_custom_call" | custom-call | tf_op jit(solution)/shard_map/tile_turns/pallas_call | solution.py:365
  33.0 0.0 copy-done
  33.0 24.8 %sum_phi.1 = f32[8,512]{1,0:T(8,128)S(1)} custom-call(f32[4,8,4,2,8,512]{5,4,3,2,1,0:T(8,128)S(1)} %bitcast.3, f32[8,512]{1,0:T(8,128)S(1)} %copy-done, f32[8,128]{1,0:T(8,128)S(1)} %get-tuple-element.16.total_ref), custom_call_target="tpu_custom_call" | custom-call | tf_op jit(solution)/shard_map/sum_phi/pallas_call | solution.py:448
  57.8 0.6 %copy.9 = f32[8,512]{1,0:T(8,128)} copy(f32[8,512]{1,0:T(8,128)S(1)} %sum_phi.1) | data formatting | bytes 32768
Async XLA Ops:
  26.9 6.1 %copy-start = (f32[8,512]{1,0:T(8,128)S(1)}, f32[8,512]{1,0:T(8,128)}, u32[]{:S(2)}) copy-start(f32[8,512]{1,0:T(8,128)} %user_ref.1) | copy-start | bytes 49156

commit v6 on v5

--- a/solution.py
+++ b/solution.py
@@ -355,7 +355,11 @@
         backward(group + 1, w_odd, m_odd)
         return carry
 
-    lax.fori_loop(0, lax.shift_right_logical(groups + 1, 1), turn, 0)
+    lax.fori_loop(0, lax.shift_right_logical(groups, 1), turn, 0)
+
+    @pl.when((groups & 1) == 1)
+    def _():
+        backward(groups - 1, w_even, m_even)
 
 
 def phi_call(plan, users, items, days, counts):

time: 58.6 us -> 58.4 us (level)
  the two profiles are of different devices: /device:TPU:6 before, /device:TPU:8 now
where the time goes in v6:
time: 58.4 us; the launch traced here: 57.8 us
  Pallas kernels  56.4 us (97%)
  between operations  0.69 us (1%)
  local copies, waits for them, and re-layouts  0.61 us (1%)
    pallas_call x1, Pallas kernels, gather_call(): pl.pallas_call(gather_kernel, out_shape=(pltpu.VMEM((NX, NZ, NY, NC, ROWS...  27 us
    pallas_call x1, Pallas kernels, scatter_call(): pl.pallas_call(scatter_kernel, out_shape=jax.ShapeDtypeStruct((ROWS, R),...  22 us
    pallas_call x1, Pallas kernels, phi_call(): pl.pallas_call(phi_kernel, out_shape=pltpu.VMEM((USER_BLOCKS, TILE, R), j...  7.42 us

profile of v6, /device:TPU:8, one launch (start us, length us, event | category | flops | bytes accessed | tf_op | source)
XLA Modules:
  0.0 57.8 jit_solution(171985427455282752)
XLA Ops:
  0.7 27.0 %gather_users.1 = (bf16[4,8,4,2,8,512]{5,4,3,2,1,0:T(8,128)(2,1)S(1)}, bf16[512,512]{1,0:T(8,128)(2,1)S(1)}, f32[96,512]{1,0:T(8,128)S(1)}, bf16[192,128,128]{2,...) custom-call(f32[8,512]{1,0:T(8,128)} %user_ref.1, bf16[512,512]{1,0:T(8,128)(2,1)} %item_hbm.1, ...), custom_call_target="tpu_custom_call" | custom-call | tf_op jit(solution)/shard_map/gather_users/pallas_call | solution.py:270
  27.7 0.0 copy-start
  27.7 7.4 %tile_turns.1 = f32[16,128,512]{2,1,0:T(8,128)S(1)} custom-call(s32[8,128]{1,0:T(8,128)S(4)} %get-tuple-element.11.plan_ref, bf16[32,64,512]{2,1,0:T(8,128)(2,1)S(1)} %bitcast.4, bf16[4,128,512]{2,1,0:T(8,128)(2,1)S(1)} %bitcast.5, f32[96,512]{1,0:T(8,128)S(1)} %get-tuple-element.14.day_ref, bf16[192,128,128]{2,1,0:T(8,128)(2,1)S(1)} %get-tuple-element.15.counts_ref), custom_call_target="tpu_custom_call" | custom-call | tf_op jit(solution)/shard_map/tile_turns/pallas_call | solution.py:369
  35.1 0.0 copy-done
  35.1 22.0 %sum_phi.1 = f32[8,512]{1,0:T(8,128)S(1)} custom-call(f32[4,8,4,2,8,512]{5,4,3,2,1,0:T(8,128)S(1)} %bitcast.3, f32[8,512]{1,0:T(8,128)S(1)} %copy-done, f32[8,128]{1,0:T(8,128)S(1)} %get-tuple-element.16.total_ref), custom_call_target="tpu_custom_call" | custom-call | tf_op jit(solution)/shard_map/sum_phi/pallas_call | solution.py:452
  57.1 0.6 %copy.9 = f32[8,512]{1,0:T(8,128)} copy(f32[8,512]{1,0:T(8,128)S(1)} %sum_phi.1) | data formatting | bytes 32768
Async XLA Ops:
  27.7 7.4 %copy-start = (f32[8,512]{1,0:T(8,128)S(1)}, f32[8,512]{1,0:T(8,128)}, u32[]{:S(2)}) copy-start(f32[8,512]{1,0:T(8,128)} %user_ref.1) | copy-start | bytes 49156
